TPU v7x, 256 devices: a whole 4x4x8 slice. The times are simulated.
256 devices in a mesh: gx: 16 (over x_hi, z), gy: 4 (over y), gz: 4 (over x_lo, core).
Axes of the slice: x: 4 (x_hi: 2, x_lo: 2; x = x_hi * 2 + x_lo), y: 4, z: 8, core: 2. Of those that a mesh axis runs over, the one named last changes fastest.
Arguments:
- scalar_field: float32 [64, 1536, 1536], P('gx', 'gy', 'gz'), may hold values from 0 to 1
- materials: int32 [64, 1536, 1536], P('gx', 'gy', 'gz'), may hold values from 0 to 7
- transfer_table: float32 [4, 128], replicated, may hold values from 0.1 to 3
- material_gain: float32 [4, 8], replicated, may hold values from 0.3 to 3
- depth_order_x: int32 [4, 4, 16], replicated, may hold values from 0 to 15, each once within a row
- depth_order_y: int32 [4], replicated, may hold values from 0 to 3, each once
- depth_order_z: int32 [4], replicated, may hold values from 0 to 3, each once
Outputs:
- frame_along_x: float32 [4, 4, 16, 24, 1536], P(None, 'gy', 'gx', None, 'gz')
- frame_along_y: float32 [4, 64, 1536], P(None, 'gx', 'gz')
- frame_along_z: float32 [4, 64, 1536], P(None, 'gx', 'gy')
Inputs may be any that keep to these rules, and one draw needn't show every extreme that they name: `depth_order_x`: entry [a, b, k] names the x slab that lies k-th from the viewer in the frame tile of y slab a and z slab b; every slab once in each tile. `depth_order_y`: entry k names the slab that lies k-th from the viewer; every slab once. `depth_order_z`: entry k names the slab that lies k-th from the viewer; every slab once.
All inputs are finite; a program needn't handle non-finite values.
Results may differ from a plain program's by a relative error of at most 0.0003.
Values sent between devices are 32-bit elements; how exact they have to be, the bound alone decides.
No kernel may reach another device: no remote copies, remote signals or barrier semaphores. Data moves between devices by JAX's collectives and lax.ppermute only.
A program may use at most 128 MiB of HBM per device.

v0:
```python
import jax
import jax.numpy as jnp
from jax import lax
from jax.sharding import PartitionSpec as P


def classify_cells(scalar_field, materials, transfer_table, material_gain):
    brick_shape = scalar_field.shape
    cell_count = scalar_field.size
    block_size = min(cell_count, 32768)
    block_count = cell_count // block_size
    bin_count = transfer_table.shape[1]
    kind_count = material_gain.shape[1]
    levels = lax.broadcasted_iota(jnp.float32, (bin_count, 1), 0)
    labels = lax.broadcasted_iota(jnp.int32, (kind_count, 1), 0)

    def one_block(pair):
        values, mark_block = pair
        scaled = values[None, :] * (bin_count - 1.0)
        weights = jnp.maximum(0.0, 1.0 - jnp.abs(scaled - levels))
        sample = jnp.dot(
            transfer_table,
            weights,
            precision=lax.Precision.HIGHEST,
            preferred_element_type=jnp.float32,
        )
        chosen = (mark_block[None, :] == labels).astype(jnp.float32)
        gain_cols = jnp.dot(
            material_gain,
            chosen,
            precision=lax.Precision.HIGHEST,
            preferred_element_type=jnp.float32,
        )
        return sample * gain_cols

    classes = lax.map(
        one_block,
        (scalar_field.reshape(block_count, block_size), materials.reshape(block_count, block_size)),
    )
    return jnp.transpose(classes, (1, 0, 2)).reshape((4,) + brick_shape)


def march(classes, march_dim, step_size):
    emission = classes[0:3]
    extinction = classes[3]
    before = jnp.cumsum(extinction, axis=march_dim) - extinction
    opacity = 1.0 - jnp.exp(-step_size * extinction)
    weights = jnp.exp(-step_size * before) * opacity
    colour = jnp.sum(weights[None] * emission, axis=march_dim + 1)
    through = jnp.exp(-step_size * jnp.sum(extinction, axis=march_dim))
    return jnp.concatenate([colour, through[None]], axis=0)


def composite(slab_list, depth_order):
    ranked = jnp.take(slab_list, depth_order, axis=0)
    through = ranked[:, 3]
    front_side = jnp.cumprod(through, axis=0)
    before = jnp.concatenate([jnp.ones_like(front_side[:1]), front_side[:-1]], axis=0)
    colour = jnp.sum(before[:, None] * ranked[:, 0:3], axis=0)
    return jnp.concatenate([colour, front_side[-1][None]], axis=0)


def shards(
    scalar_field,
    materials,
    transfer_table,
    material_gain,
    depth_order_x,
    depth_order_y,
    depth_order_z,
):
    cells_x, cells_y, cells_z = scalar_field.shape
    step_x = 1.0 / (cells_x * lax.axis_size("gx"))
    step_y = 1.0 / (cells_y * lax.axis_size("gy"))
    step_z = 1.0 / (cells_z * lax.axis_size("gz"))
    classes = classify_cells(scalar_field, materials, transfer_table, material_gain)
    image_x = march(classes, 0, step_x)
    image_y = march(classes, 1, step_y)
    image_z = march(classes, 2, step_z)
    tile_order = depth_order_x[lax.axis_index("gy"), lax.axis_index("gz")]
    frame_piece = composite(
        lax.all_to_all(image_x[None], "gx", split_axis=2, concat_axis=0, tiled=True), tile_order
    )
    frame_along_x = frame_piece[:, None, None]
    gathered_y = lax.all_gather(image_y[None], "gy", axis=0, tiled=True)
    frame_along_y = composite(gathered_y, depth_order_y)
    gathered_z = lax.all_gather(image_z[None], "gz", axis=0, tiled=True)
    frame_along_z = composite(gathered_z, depth_order_z)
    return (frame_along_x, frame_along_y, frame_along_z)


def solution(mesh):
    return jax.shard_map(
        shards,
        mesh=mesh,
        in_specs=(P("gx", "gy", "gz"), P("gx", "gy", "gz"), P(), P(), P(), P(), P()),
        out_specs=(P(None, "gy", "gx", None, "gz"), P(None, "gx", "gz"), P(None, "gx", "gy")),
        check_vma=False,
    )
```

profile of v0, /device:TPU:16, one launch (start us, length us, event | category | flops | bytes accessed | tf_op | source)
XLA Modules:
  0.0 503.7 jit_solution(12011562297537679570)
XLA Ops:
  0.6 2.3 reshape.163
  3.0 4.0 reshape.164
  6.9 347.8 %while.11 = (s32[]{:T(128)}, f32[18,4,32768]{2,1,0:T(4,128)}, f32[18,32768]{1,0:T(8,128)S(1)}, f32[4,128]{1,0:T(4,128)S(1)}, s32[18,32768]{1,0:T(8,128)}, /*index=5*/f32[4,8]{1,0:T(4,128)S(1)}, s32[]{:T(128)}) while((s32[]{:T(128)}, f32[18,4,32768]{2,1,0:T(4,128)}, f32[18,32768]{1,0:T(8,128)S(1)}, f32[4,128]{1,0:T(4,128)S(1)}, ...), condition=%wide.region_1.2_spmd.clone, body=%wide.region_0.1_spmd.clone.sunk | while | flops 231112704 | bytes 2362069 | solution.py:36
  7.1 16.5 %fusion.43 = f32[32768,4]{0,1:T(4,128)S(1)} fusion(f32[4,128]{1,0:T(4,128)S(1)} %get-tuple-element.141, f32[32768]{0:T(1024)S(1)} %bitcast.82), kind=kOutput, calls=%fused_computation.12.clone.1 | convolution fusion | flops 218103808 | bytes 657408 | tf_op jit(solution)/shard_map/while/body/eval_jaxpr/dot_general | solution.py:21
  26.4 16.5 %fusion.43 = f32[32768,4]{0,1:T(4,128)S(1)} fusion(f32[4,128]{1,0:T(4,128)S(1)} %get-tuple-element.141, f32[32768]{0:T(1024)S(1)} %bitcast.82), kind=kOutput, calls=%fused_computation.12.clone.1 | convolution fusion | flops 218103808 | bytes 657408 | tf_op jit(solution)/shard_map/while/body/eval_jaxpr/dot_general | solution.py:21
  45.7 16.5 %fusion.43 = f32[32768,4]{0,1:T(4,128)S(1)} fusion(f32[4,128]{1,0:T(4,128)S(1)} %get-tuple-element.141, f32[32768]{0:T(1024)S(1)} %bitcast.82), kind=kOutput, calls=%fused_computation.12.clone.1 | convolution fusion | flops 218103808 | bytes 657408 | tf_op jit(solution)/shard_map/while/body/eval_jaxpr/dot_general | solution.py:21
  65.0 16.5 %fusion.43 = f32[32768,4]{0,1:T(4,128)S(1)} fusion(f32[4,128]{1,0:T(4,128)S(1)} %get-tuple-element.141, f32[32768]{0:T(1024)S(1)} %bitcast.82), kind=kOutput, calls=%fused_computation.12.clone.1 | convolution fusion | flops 218103808 | bytes 657408 | tf_op jit(solution)/shard_map/while/body/eval_jaxpr/dot_general | solution.py:21
  84.3 16.5 %fusion.43 = f32[32768,4]{0,1:T(4,128)S(1)} fusion(f32[4,128]{1,0:T(4,128)S(1)} %get-tuple-element.141, f32[32768]{0:T(1024)S(1)} %bitcast.82), kind=kOutput, calls=%fused_computation.12.clone.1 | convolution fusion | flops 218103808 | bytes 657408 | tf_op jit(solution)/shard_map/while/body/eval_jaxpr/dot_general | solution.py:21
  103.6 16.5 %fusion.43 = f32[32768,4]{0,1:T(4,128)S(1)} fusion(f32[4,128]{1,0:T(4,128)S(1)} %get-tuple-element.141, f32[32768]{0:T(1024)S(1)} %bitcast.82), kind=kOutput, calls=%fused_computation.12.clone.1 | convolution fusion | flops 218103808 | bytes 657408 | tf_op jit(solution)/shard_map/while/body/eval_jaxpr/dot_general | solution.py:21
  123.0 16.5 %fusion.43 = f32[32768,4]{0,1:T(4,128)S(1)} fusion(f32[4,128]{1,0:T(4,128)S(1)} %get-tuple-element.141, f32[32768]{0:T(1024)S(1)} %bitcast.82), kind=kOutput, calls=%fused_computation.12.clone.1 | convolution fusion | flops 218103808 | bytes 657408 | tf_op jit(solution)/shard_map/while/body/eval_jaxpr/dot_general | solution.py:21
  142.3 16.5 %fusion.43 = f32[32768,4]{0,1:T(4,128)S(1)} fusion(f32[4,128]{1,0:T(4,128)S(1)} %get-tuple-element.141, f32[32768]{0:T(1024)S(1)} %bitcast.82), kind=kOutput, calls=%fused_computation.12.clone.1 | convolution fusion | flops 218103808 | bytes 657408 | tf_op jit(solution)/shard_map/while/body/eval_jaxpr/dot_general | solution.py:21
  161.6 16.5 %fusion.43 = f32[32768,4]{0,1:T(4,128)S(1)} fusion(f32[4,128]{1,0:T(4,128)S(1)} %get-tuple-element.141, f32[32768]{0:T(1024)S(1)} %bitcast.82), kind=kOutput, calls=%fused_computation.12.clone.1 | convolution fusion | flops 218103808 | bytes 657408 | tf_op jit(solution)/shard_map/while/body/eval_jaxpr/dot_general | solution.py:21
  180.9 16.5 %fusion.43 = f32[32768,4]{0,1:T(4,128)S(1)} fusion(f32[4,128]{1,0:T(4,128)S(1)} %get-tuple-element.141, f32[32768]{0:T(1024)S(1)} %bitcast.82), kind=kOutput, calls=%fused_computation.12.clone.1 | convolution fusion | flops 218103808 | bytes 657408 | tf_op jit(solution)/shard_map/while/body/eval_jaxpr/dot_general | solution.py:21
  200.2 16.5 %fusion.43 = f32[32768,4]{0,1:T(4,128)S(1)} fusion(f32[4,128]{1,0:T(4,128)S(1)} %get-tuple-element.141, f32[32768]{0:T(1024)S(1)} %bitcast.82), kind=kOutput, calls=%fused_computation.12.clone.1 | convolution fusion | flops 218103808 | bytes 657408 | tf_op jit(solution)/shard_map/while/body/eval_jaxpr/dot_general | solution.py:21
  219.6 16.5 %fusion.43 = f32[32768,4]{0,1:T(4,128)S(1)} fusion(f32[4,128]{1,0:T(4,128)S(1)} %get-tuple-element.141, f32[32768]{0:T(1024)S(1)} %bitcast.82), kind=kOutput, calls=%fused_computation.12.clone.1 | convolution fusion | flops 218103808 | bytes 657408 | tf_op jit(solution)/shard_map/while/body/eval_jaxpr/dot_general | solution.py:21
  238.9 16.5 %fusion.43 = f32[32768,4]{0,1:T(4,128)S(1)} fusion(f32[4,128]{1,0:T(4,128)S(1)} %get-tuple-element.141, f32[32768]{0:T(1024)S(1)} %bitcast.82), kind=kOutput, calls=%fused_computation.12.clone.1 | convolution fusion | flops 218103808 | bytes 657408 | tf_op jit(solution)/shard_map/while/body/eval_jaxpr/dot_general | solution.py:21
  258.2 16.5 %fusion.43 = f32[32768,4]{0,1:T(4,128)S(1)} fusion(f32[4,128]{1,0:T(4,128)S(1)} %get-tuple-element.141, f32[32768]{0:T(1024)S(1)} %bitcast.82), kind=kOutput, calls=%fused_computation.12.clone.1 | convolution fusion | flops 218103808 | bytes 657408 | tf_op jit(solution)/shard_map/while/body/eval_jaxpr/dot_general | solution.py:21
  277.5 16.5 %fusion.43 = f32[32768,4]{0,1:T(4,128)S(1)} fusion(f32[4,128]{1,0:T(4,128)S(1)} %get-tuple-element.141, f32[32768]{0:T(1024)S(1)} %bitcast.82), kind=kOutput, calls=%fused_computation.12.clone.1 | convolution fusion | flops 218103808 | bytes 657408 | tf_op jit(solution)/shard_map/while/body/eval_jaxpr/dot_general | solution.py:21
  296.8 16.5 %fusion.43 = f32[32768,4]{0,1:T(4,128)S(1)} fusion(f32[4,128]{1,0:T(4,128)S(1)} %get-tuple-element.141, f32[32768]{0:T(1024)S(1)} %bitcast.82), kind=kOutput, calls=%fused_computation.12.clone.1 | convolution fusion | flops 218103808 | bytes 657408 | tf_op jit(solution)/shard_map/while/body/eval_jaxpr/dot_general | solution.py:21
  316.2 16.5 %fusion.43 = f32[32768,4]{0,1:T(4,128)S(1)} fusion(f32[4,128]{1,0:T(4,128)S(1)} %get-tuple-element.141, f32[32768]{0:T(1024)S(1)} %bitcast.82), kind=kOutput, calls=%fused_computation.12.clone.1 | convolution fusion | flops 218103808 | bytes 657408 | tf_op jit(solution)/shard_map/while/body/eval_jaxpr/dot_general | solution.py:21
  333.9 1.4 fusion.44
  335.5 16.5 %fusion.43 = f32[32768,4]{0,1:T(4,128)S(1)} fusion(f32[4,128]{1,0:T(4,128)S(1)} %get-tuple-element.141, f32[32768]{0:T(1024)S(1)} %bitcast.82), kind=kOutput, calls=%fused_computation.12.clone.1 | convolution fusion | flops 218103808 | bytes 657408 | tf_op jit(solution)/shard_map/while/body/eval_jaxpr/dot_general | solution.py:21
  353.3 1.5 fusion.44
  354.8 12.2 %slice_reduce_fusion = f32[18,32768]{1,0:T(8,128)} fusion(f32[4,18,32768]{2,0,1:T(4,128)} %bitcast.1), kind=kLoop, calls=%fused_computation.27 | loop fusion | bytes 4718592 | tf_op jit(solution)/shard_map/slice | solution.py:45
  367.0 2.6 reduce_window_sum.47
  369.6 4.7 reshape.167
  374.3 2.1 subtract_multiply_fusion
  376.4 1.6 fusion.17
  378.0 1.7 copy-done.2
  379.8 2.6 broadcast_add_fusion.1
  382.4 1.7 copy.37
  384.1 4.7 copy.38
  388.8 2.5 fusion.30
  391.2 1.6 copy-done.1
  392.9 2.4 broadcast_add_fusion
  395.3 1.6 copy.39
  397.0 3.1 copy.40
  400.1 11.5 %copy.32 = f32[3,18,32768]{2,1,0:T(8,128)} copy(f32[3,18,32768]{2,0,1:T(4,128)} %bitcast.66) | data formatting | bytes 14155776 | tf_op jit(solution)/shard_map/slice | solution.py:44
  411.6 8.4 %slice.64 = f32[3,4,384,384]{3,2,1,0:T(8,128)} reshape(f32[3,18,32768]{2,1,0:T(8,128)} %copy.32) | data formatting | bytes 14155776 | tf_op jit(solution)/shard_map/slice | solution.py:44
  420.0 4.0 fusion.21
  425.1 2.5 multiply_reduce_fusion
  427.8 2.9 copy.33
  430.7 11.2 %all-to-all-start = ((f32[1,4,384,384]{3,1,0,2:T(4,128)}), f32[1,4,384,384]{3,1,0,2:T(4,128)S(1)}, u32[]{:S(2)}, u32[]{:S(2)}) async-start(f32[1,4,384,384]{3,1,0,2:T(4,128)} %copy.33), calls=%async_computation | async-start | bytes 4718592 | tf_op jit(solution)/shard_map/all_to_all | solution.py:82
  441.9 6.6 %all-gather.1 = f32[16,4,384]{2,1,0:T(4,128)S(1)} all-gather(f32[4,4,384]{2,1,0:T(4,128)S(1)} %pad_maximum_fusion.2), channel_id=3, replica_groups=mesh['gx'=16,'gy'=4,'gz'=4] {'gz'}, dimensions={0}, use_global_device_ids=true | all-gather | bytes 122880 | tf_op jit(solution)/shard_map/all_gather | solution.py:87
  449.3 10.7 %all-gather = f32[16,4,384]{2,1,0:T(4,128)S(1)} all-gather(f32[4,4,384]{2,1,0:T(4,128)S(1)} %pad_maximum_fusion), channel_id=2, replica_groups=mesh['gx'=16,'gy'=4,'gz'=4] {'gy'}, dimensions={0}, use_global_device_ids=true | all-gather | bytes 122880 | tf_op jit(solution)/shard_map/all_gather | solution.py:85
  462.9 35.4 %all-to-all-done = f32[1,4,384,384]{3,1,0,2:T(4,128)S(1)} async-done(((f32[1,4,384,384]{3,1,0,2:T(4,128)}), f32[1,4,384,384]{3,1,0,2:T(4,128)S(1)}, u32[]{:S(2)}, u32[]{:S(2)}) %all-to-all-start) | async-done | bytes 2359328 | tf_op jit(solution)/shard_map/all_to_all | solution.py:82
  498.4 1.6 copy.46
  499.9 2.4 gather_fusion
  (108 shorter events, 54.7 us)
Async XLA Ops:
  3.0 4.0 copy-start.4
  3.0 4.0 copy-start.5
  378.0 1.7 copy-start.2
  391.2 1.6 copy-start.1
  420.0 4.4 copy-start
  420.0 5.1 %copy-start.3 = (f32[4,384,384]{2,1,0:T(8,128)S(1)}, f32[4,384,384]{2,1,0:T(8,128)}, u32[]{:S(2)}) copy-start(f32[4,384,384]{2,1,0:T(8,128)} %subtract_multiply_fusion) | copy-start | bytes 7077892
  430.7 17.8 %copy-start.6 = (s32[4]{0:T(128)S(1)}, s32[4]{0:T(128)}, u32[]{:S(2)}) copy-start(s32[4]{0:T(128)} %param.17) | copy-start | bytes 52
  430.7 29.3 %copy-start.7 = (s32[4]{0:T(128)S(1)}, s32[4]{0:T(128)}, u32[]{:S(2)}) copy-start(s32[4]{0:T(128)} %param.16) | copy-start | bytes 52
  430.7 67.6 %all-to-all-start = ((f32[1,4,384,384]{3,1,0,2:T(4,128)}), f32[1,4,384,384]{3,1,0,2:T(4,128)S(1)}, u32[]{:S(2)}, u32[]{:S(2)}) async-start(f32[1,4,384,384]{3,1,0,2:T(4,128)} %copy.33), calls=%async_computation | async-start | bytes 4718592 | tf_op jit(solution)/shard_map/all_to_all | solution.py:82
where the time goes:
time: 505 us; the launch traced here: 504 us
  matrix products  322 us (64%)
  local copies, waits for them, and re-layouts  93.2 us (18%)
  waiting for transfers between devices  35.4 us (7%)
  other arithmetic  23.8 us (5%)
  blocking collectives  17.3 us (3%)
  starting transfers between devices  11.2 us (2%)
    dot_general x18, matrix products, one_block(): jnp.dot(transfer_table, weights, precision=lax.Precision.HIGHEST, preferr...  296 us
    all_to_all x1, waiting for transfers between devices, shards(): lax.all_to_all(image_x[None], 'gx', split_axis=2, concat_axis=0, tiled=True)  35.4 us
    dot_general x18, matrix products, one_block(): jnp.dot(material_gain, chosen, precision=lax.Precision.HIGHEST, preferred...  25.4 us
    dynamic_slice x18, local copies, waits for them, and re-layouts, classify_cells(): lax.map(one_block, (scalar_field.reshape(block_count, block_size), materi...  23.8 us
    slice x2, local copies, waits for them, and re-layouts, march(): emission = classes[0:3]  19.9 us
    another operation x7, local copies, waits for them, and re-layouts  15.8 us
    slice x1, local copies, waits for them, and re-layouts, march(): extinction = classes[3]  12.2 us
    all_to_all x1, starting transfers between devices, shards(): lax.all_to_all(image_x[None], 'gx', split_axis=2, concat_axis=0, tiled=True)  11.2 us
  transfers between devices with their start and end apart: 1, of which 1 were waited for; matrix products, arithmetic and copies ran while one was open for 1% of the time, Pallas kernels for 0%

commit v1 on v0

v1 whole, which is shorter than its diff:
```python
import functools, math
import jax
import jax.numpy as jnp
from jax import lax
from jax.experimental import pallas as pl
from jax.experimental.pallas import tpu as pltpu
from jax.sharding import PartitionSpec as P

LOG2E = math.log2(math.e)


def look_up(table, index):
    return jnp.take_along_axis(table, index, axis=1, mode="promise_in_bounds")


def make_tables(transfer_ref, tables_ref):
    bins = transfer_ref.shape[1]
    lane = lax.broadcasted_iota(jnp.int32, (8, 128), 1)
    for c in range(4):
        value = jnp.broadcast_to(transfer_ref[pl.ds(c, 1), :], (8, bins))
        tables_ref[c] = value
        tables_ref[4 + c] = jnp.where(lane == bins - 1, 0.0, pltpu.roll(value, bins - 1, 1) - value)


def classify(cells, marks, tables, gain_ref):
    scaled = cells * (tables[0].shape[1] - 1.0)
    lower = scaled.astype(jnp.int32)
    fraction = scaled - lower.astype(jnp.float32)
    values = [look_up(tables[c], lower) for c in range(4)]
    slopes = [look_up(tables[4 + c], lower) for c in range(4)]
    bits = [marks & (1 << k) != 0 for k in range((gain_ref.shape[1] - 1).bit_length())]
    out = []
    for c in range(4):
        gains = [gain_ref[c, k] for k in range(gain_ref.shape[1])]
        for bit in bits:
            gains = [jnp.where(bit, high, low) for low, high in zip(gains[0::2], gains[1::2])]
        out.append((values[c] + fraction * slopes[c]) * gains[0])
    return out


def x_kernel(step, field_ref, mark_ref, transfer_ref, gain_ref, out_ref, tables_ref):
    @pl.when(pl.program_id(0) == 0)
    def _():
        make_tables(transfer_ref, tables_ref)

    tables = [tables_ref[k] for k in range(8)]
    depth, rows, cols = field_ref.shape
    piece_rows = out_ref.shape[2]
    for piece in range(out_ref.shape[0]):
        for col in range(0, cols, 128):
            for row in range(0, piece_rows, 8):
                colour = None
                for x in range(depth):
                    at = (x, pl.ds(piece * piece_rows + row, 8), pl.ds(col, 128))
                    red, green, blue, extinction = classify(field_ref[at], mark_ref[at], tables, gain_ref)
                    passed = jnp.exp(extinction * -step)
                    opacity = 1.0 - passed
                    if colour is None:
                        colour = [opacity * v for v in (red, green, blue)]
                        through = passed
                    else:
                        weight = through * opacity
                        colour = [a + weight * v for a, v in zip(colour, (red, green, blue))]
                        through = through * passed
                for c, v in enumerate(colour + [through]):
                    out_ref[piece, c, pl.ds(row, 8), pl.ds(col, 128)] = v


def x_view(field, marks, transfer_table, material_gain, step, pieces, per_step=4):
    depth, rows, cols = field.shape
    piece_rows = rows // pieces
    block = pl.BlockSpec((depth, per_step * piece_rows, cols), lambda i: (0, i, 0))
    return pl.pallas_call(
        functools.partial(x_kernel, step),
        grid=(pieces // per_step,),
        in_specs=[
            block,
            block,
            pl.BlockSpec(transfer_table.shape, lambda i: (0, 0)),
            pl.BlockSpec(memory_space=pltpu.SMEM),
        ],
        out_specs=pl.BlockSpec((per_step, 4, piece_rows, cols), lambda i: (i, 0, 0, 0)),
        out_shape=jax.ShapeDtypeStruct((pieces, 4, piece_rows, cols), jnp.float32),
        scratch_shapes=[pltpu.VMEM((8, 8, 128), jnp.float32)],
        name="x_view",
    )(field, marks, transfer_table, material_gain)


def join_rows(colour, through):
    total = [v[0:1] for v in colour]
    front = through[0:1]
    for s in range(1, 8):
        total = [t + front * v[s : s + 1] for t, v in zip(total, colour)]
        front = front * through[s : s + 1]
    return total + [front]


def add_cell(state, passed, emission):
    red, green, blue, through = state
    weight = through * (1.0 - passed)
    return (
        red + weight * emission[0],
        green + weight * emission[1],
        blue + weight * emission[2],
        through * passed,
    )


def start_state():
    zero = jnp.zeros((8, 128), jnp.float32)
    return (zero, zero, zero, jnp.ones((8, 128), jnp.float32))


def yz_kernel(step, field_ref, mark_ref, transfer_ref, gain_ref, y_ref, z_ref, tables_ref, cell_ref, turned_ref):
    tile = pl.program_id(1)

    @pl.when((pl.program_id(0) == 0) & (tile == 0))
    def _():
        make_tables(transfer_ref, tables_ref)

    tables = [tables_ref[k] for k in range(8)]
    rows = field_ref.shape[1]
    run = rows // 8

    def along_y(j, state):
        at = pl.ds(j, 8, stride=run)
        red, green, blue, extinction = classify(field_ref[0, at, :], mark_ref[0, at, :], tables, gain_ref)
        passed = jnp.exp(extinction * -step)
        for c, v in enumerate((red, green, blue, passed)):
            cell_ref[c, at, :] = v
        return add_cell(state, passed, (red, green, blue))

    state = lax.fori_loop(0, run, along_y, start_state(), unroll=16)
    for c, v in enumerate(join_rows(state[:3], state[3])):
        y_ref[0, c, :] = v[0]

    to = pl.ds(pl.multiple_of(tile * 128, 128), 128)
    for c in range(4):
        for k in range(rows // 128):
            turned_ref[c, k, to, :] = cell_ref[c, pl.ds(k * 128, 128), :].T

    @pl.when(tile == pl.num_programs(1) - 1)
    def _():
        length = turned_ref.shape[2]
        run = length // 8
        for k in range(turned_ref.shape[1]):

            def along_z(j, state):
                at = pl.ds(j, 8, stride=run)
                red, green, blue, passed = [turned_ref[c, k, at, :] for c in range(4)]
                return add_cell(state, passed, (red, green, blue))

            state = lax.fori_loop(0, run, along_z, start_state(), unroll=8)
            for c, v in enumerate(join_rows(state[:3], state[3])):
                z_ref[0, c, pl.ds(k * 128, 128)] = v[0]


def yz_views(field, marks, transfer_table, material_gain, step):
    depth, rows, cols = field.shape
    block = pl.BlockSpec((1, rows, 128), lambda i, j: (i, 0, j))
    return pl.pallas_call(
        functools.partial(yz_kernel, step),
        grid=(depth, cols // 128),
        in_specs=[
            block,
            block,
            pl.BlockSpec(transfer_table.shape, lambda i, j: (0, 0)),
            pl.BlockSpec(memory_space=pltpu.SMEM),
        ],
        out_specs=[
            pl.BlockSpec((1, 4, 128), lambda i, j: (i, 0, j)),
            pl.BlockSpec((1, 4, rows), lambda i, j: (i, 0, 0)),
        ],
        out_shape=[
            jax.ShapeDtypeStruct((depth, 4, cols), jnp.float32),
            jax.ShapeDtypeStruct((depth, 4, rows), jnp.float32),
        ],
        scratch_shapes=[
            pltpu.VMEM((8, 8, 128), jnp.float32),
            pltpu.VMEM((4, rows, 128), jnp.float32),
            pltpu.VMEM((4, rows // 128, cols, 128), jnp.float32),
        ],
        name="yz_views",
    )(field, marks, transfer_table, material_gain)


def x_frame_kernel(order_ref, part_ref, out_ref):
    slabs = part_ref.shape[0]
    first = part_ref.at[order_ref[0]]
    total = [first[c] for c in range(3)]
    front = first[3]
    for k in range(1, slabs):
        part = part_ref.at[order_ref[k]]
        total = [t + front * part[c] for c, t in enumerate(total)]
        front = front * part[3]
    for c, v in enumerate(total + [front]):
        out_ref[c] = v


def x_frame(parts, order):
    return pl.pallas_call(
        x_frame_kernel,
        in_specs=[pl.BlockSpec(memory_space=pltpu.SMEM), pl.BlockSpec(memory_space=pltpu.VMEM)],
        out_specs=pl.BlockSpec(memory_space=pltpu.VMEM),
        out_shape=jax.ShapeDtypeStruct(parts.shape[1:], jnp.float32),
        name="x_frame",
    )(order, parts)


def yz_frame_kernel(y_order_ref, z_order_ref, y_part_ref, z_part_ref, y_out_ref, z_out_ref):
    for order_ref, part_ref, out_ref in (
        (y_order_ref, y_part_ref, y_out_ref),
        (z_order_ref, z_part_ref, z_out_ref),
    ):
        slabs, depth, _, cols = part_ref.shape
        for x in range(depth):
            first = part_ref.at[order_ref[0], x]
            total = [first[pl.ds(c, 1), :] for c in range(3)]
            front = first[pl.ds(3, 1), :]
            for k in range(1, slabs):
                part = part_ref.at[order_ref[k], x]
                total = [t + front * part[pl.ds(c, 1), :] for c, t in enumerate(total)]
                front = front * part[pl.ds(3, 1), :]
            for c, v in enumerate(total + [front]):
                out_ref[c, pl.ds(x, 1), :] = v


def yz_frames(y_parts, z_parts, y_order, z_order):
    smem = pl.BlockSpec(memory_space=pltpu.SMEM)
    vmem = pl.BlockSpec(memory_space=pltpu.VMEM)
    shape = lambda parts: jax.ShapeDtypeStruct((4, parts.shape[1], parts.shape[3]), jnp.float32)
    return pl.pallas_call(
        yz_frame_kernel,
        in_specs=[smem, smem, vmem, vmem],
        out_specs=[vmem, vmem],
        out_shape=[shape(y_parts), shape(z_parts)],
        name="yz_frames",
    )(y_order, z_order, y_parts, z_parts)


def shards(scalar_field, materials, transfer_table, material_gain, depth_order_x, depth_order_y, depth_order_z):
    cells_x, cells_y, cells_z = scalar_field.shape
    pieces = lax.axis_size("gx")
    step_x = 1.0 / (cells_x * pieces)
    step_y = 1.0 / (cells_y * lax.axis_size("gy"))
    step_z = 1.0 / (cells_z * lax.axis_size("gz"))
    assert step_y == step_z
    image_x = x_view(scalar_field, materials, transfer_table, material_gain, step_x, pieces)
    parts_x = lax.all_to_all(image_x, "gx", split_axis=0, concat_axis=0, tiled=True)
    image_y, image_z = yz_views(scalar_field, materials, transfer_table, material_gain, step_y)
    parts_y = lax.all_gather(image_y, "gy", axis=0)
    parts_z = lax.all_gather(image_z, "gz", axis=0)
    frame_y, frame_z = yz_frames(parts_y, parts_z, depth_order_y, depth_order_z)
    tile_order = depth_order_x[lax.axis_index("gy"), lax.axis_index("gz")]
    frame_x = x_frame(parts_x, tile_order)
    return frame_x[:, None, None], frame_y, frame_z


def solution(mesh):
    return jax.shard_map(
        shards,
        mesh=mesh,
        in_specs=(P("gx", "gy", "gz"), P("gx", "gy", "gz"), P(), P(), P(), P(), P()),
        out_specs=(P(None, "gy", "gx", None, "gz"), P(None, "gx", "gz"), P(None, "gx", "gy")),
        check_vma=False,
    )
```

time: 505 us -> 82.5 us (0.16)
  matrix products: 322 us -> 0 us
  local copies, waits for them, and re-layouts: 93.2 us -> 2 us
  Pallas kernels: 0 us -> 33.5 us
  other arithmetic: 23.8 us -> 0 us
  waiting for transfers between devices: 35.4 us -> 14.5 us
    dot_general x36 -> x0, matrix products: 322 us -> none  [the longest x18 296 us: one_block(): jnp.dot(transfer_table, weights, precision=lax.Precision.HIGHEST, preferr...]
    pallas_call x0 -> x4, Pallas kernels: none -> 33.5 us  [the longest x1 19.9 us: yz_views(): pl.pallas_call(functools.partial(yz_kernel, step), grid=(depth, cols // 1...]
    slice x9 -> x0, local copies, waits for them, and re-layouts: 32.2 us -> none  [the longest x2 19.9 us: march(): emission = classes[0:3]]
    dynamic_slice x18 -> x0, local copies, waits for them, and re-layouts: 23.8 us -> none  [classify_cells(): lax.map(one_block, (scalar_field.reshape(block_count, block_size), materi...]
    all_to_all x1, waiting for transfers between devices: 35.4 us -> 14.5 us  [shards(): lax.all_to_all(image_x, 'gx', split_axis=0, concat_axis=0, tiled=True)]
    another operation x8 -> x0, local copies, waits for them, and re-layouts: 18.4 us -> none
    another operation x10 -> x0, other arithmetic: 11.5 us -> none
    reshape x2 -> x0, local copies, waits for them, and re-layouts: 6.26 us -> none  [the longest x1 3.96 us: classify_cells(): materials.reshape(block_count, block_size)]
  transfers between devices with their start and end apart: 1 -> 1, of which waited for: 1 -> 1; matrix products, arithmetic and copies ran while one was open for 1% -> 1% of each run, Pallas kernels for 0% -> 26%
where the time goes in v1:
time: 82.5 us; the launch traced here: 82.1 us
  Pallas kernels  33.5 us (41%)
  blocking collectives  20.4 us (25%)
  waiting for transfers between devices  14.5 us (18%)
  starting transfers between devices  11 us (13%)
  local copies, waits for them, and re-layouts  2 us (2%)
    pallas_call x1, Pallas kernels, yz_views(): pl.pallas_call(functools.partial(yz_kernel, step), grid=(depth, cols // 1...  19.9 us
    all_to_all x1, waiting for transfers between devices, shards(): lax.all_to_all(image_x, 'gx', split_axis=0, concat_axis=0, tiled=True)  14.5 us
    all_gather x1, blocking collectives, shards(): parts_y = lax.all_gather(image_y, 'gy', axis=0)  12.3 us
    all_to_all x1, starting transfers between devices, shards(): lax.all_to_all(image_x, 'gx', split_axis=0, concat_axis=0, tiled=True)  11 us
    pallas_call x1, Pallas kernels, x_view(): pl.pallas_call(functools.partial(x_kernel, step), grid=(pieces // per_ste...  9.42 us
    all_gather x1, blocking collectives, shards(): parts_z = lax.all_gather(image_z, 'gz', axis=0)  8.15 us
    pallas_call x1, Pallas kernels, x_frame(): pl.pallas_call(x_frame_kernel, in_specs=[pl.BlockSpec(memory_space=pltpu....  2.53 us
  transfers between devices with their start and end apart: 1, of which 1 were waited for; matrix products, arithmetic and copies ran while one was open for 1% of the time, Pallas kernels for 26%

profile of v1, /device:TPU:16, one launch (start us, length us, event | category | flops | bytes accessed | tf_op | source)
XLA Modules:
  0.0 82.1 jit_solution(1638426959713301957)
XLA Ops:
  0.6 0.0 copy-start
  0.6 9.4 %x_view.1 = f32[16,4,24,384]{3,2,1,0:T(8,128)} custom-call(f32[4,384,384]{2,1,0:T(8,128)} %field_ref.3, s32[4,384,384]{2,1,0:T(8,128)} %mark_ref.3, f32[4,128]{1,0:T(4,128)} %transfer_ref.3, f32[4,8]{1,0:T(4,128)} %gain_ref.3), custom_call_target="tpu_custom_call" | custom-call | tf_op jit(solution)/shard_map/x_view/pallas_call | solution.py:73
  10.1 11.0 %all-to-all-start = ((f32[16,4,24,384]{3,2,1,0:T(8,128)}), f32[16,4,24,384]{3,2,1,0:T(8,128)S(1)}, u32[]{:S(2)}, u32[]{:S(2)}) async-start(f32[16,4,24,384]{3,2,1,0:T(8,128)} %x_view.1), calls=%async_computation | async-start | bytes 4718592 | tf_op jit(solution)/shard_map/all_to_all | solution.py:249
  21.1 19.9 %yz_views.1 = (f32[4,4,384]{2,1,0:T(4,128)}, f32[4,4,384]{2,1,0:T(4,128)}) custom-call(f32[4,384,384]{2,1,0:T(8,128)} %field_ref.3, s32[4,384,384]{2,1,0:T(8,128)} %mark_ref.3, f32[4,128]{1,0:T(4,128)} %transfer_ref.3, f32[4,8]{1,0:T(4,128)} %gain_ref.3), custom_call_target="tpu_custom_call" | custom-call | tf_op jit(solution)/shard_map/yz_views/pallas_call | solution.py:161
  41.0 12.3 %all-gather = f32[16,4,384]{2,1,0:T(4,128)} all-gather(f32[4,4,384]{2,1,0:T(4,128)} %get-tuple-element.7), channel_id=2, replica_groups=mesh['gx'=16,'gy'=4,'gz'=4] {'gy'}, dimensions={0}, use_global_device_ids=true | all-gather | bytes 122880 | tf_op jit(solution)/shard_map/all_gather | solution.py:251
  53.3 8.2 %all-gather.1 = f32[16,4,384]{2,1,0:T(4,128)} all-gather(f32[4,4,384]{2,1,0:T(4,128)} %get-tuple-element.8), channel_id=3, replica_groups=mesh['gx'=16,'gy'=4,'gz'=4] {'gz'}, dimensions={0}, use_global_device_ids=true | all-gather | bytes 122880 | tf_op jit(solution)/shard_map/all_gather | solution.py:252
  61.4 1.6 %yz_frames.1 = (f32[4,4,384]{2,1,0:T(4,128)}, f32[4,4,384]{2,1,0:T(4,128)}) custom-call(s32[4]{0:T(128)} %y_order_ref.1, s32[4]{0:T(128)} %z_order_ref.1, f32[4,4,4,384]{3,2,1,0:T(4,128)} %bitcast.7, f32[4,4,4,384]{3,2,1,0:T(4,128)} %bitcast.8), custom_call_target="tpu_custom_call" | custom-call | tf_op jit(solution)/shard_map/yz_frames/pallas_call | solution.py:232
  63.1 0.0 copy-done
  63.1 0.6 dynamic-slice_bitcast_fusion.order_ref
  63.6 14.5 %all-to-all-done.part_ref = f32[16,4,24,384]{3,2,1,0:T(8,128)S(1)} async-done(((f32[16,4,24,384]{3,2,1,0:T(8,128)}), f32[16,4,24,384]{3,2,1,0:T(8,128)S(1)}, u32[]{:S(2)}, u32[]{:S(2)}) %all-to-all-start) | async-done | bytes 2359328 | tf_op jit(solution)/shard_map/all_to_all | solution.py:249
  78.2 0.0 copy-start.1
  78.2 1.4 %copy-done.1 = f32[16,4,24,384]{3,2,1,0:T(8,128)} copy-done((f32[16,4,24,384]{3,2,1,0:T(8,128)}, f32[16,4,24,384]{3,2,1,0:T(8,128)S(1)}, u32[]{:S(2)}) %copy-start.1) | copy-done | bytes 2359320
  79.6 2.5 %x_frame.1 = f32[4,24,384]{2,1,0:T(8,128)} custom-call(s32[16]{0:T(128)} %dynamic-slice_bitcast_fusion.order_ref, f32[16,4,24,384]{3,2,1,0:T(8,128)} %copy-done.1), custom_call_target="tpu_custom_call" | custom-call | tf_op jit(solution)/shard_map/x_frame/pallas_call | solution.py:201
Async XLA Ops:
  0.6 62.4 %copy-start = (s32[4,4,16]{2,1,0:T(4,128)S(1)}, s32[4,4,16]{2,1,0:T(4,128)}, u32[]{:S(2)}) copy-start(s32[4,4,16]{2,1,0:T(4,128)} %param.11) | copy-start | bytes 3076
  10.1 68.1 %all-to-all-start = ((f32[16,4,24,384]{3,2,1,0:T(8,128)}), f32[16,4,24,384]{3,2,1,0:T(8,128)S(1)}, u32[]{:S(2)}, u32[]{:S(2)}) async-start(f32[16,4,24,384]{3,2,1,0:T(8,128)} %x_view.1), calls=%async_computation | async-start | bytes 4718592 | tf_op jit(solution)/shard_map/all_to_all | solution.py:249
  78.2 1.4 %copy-start.1 = (f32[16,4,24,384]{3,2,1,0:T(8,128)}, f32[16,4,24,384]{3,2,1,0:T(8,128)S(1)}, u32[]{:S(2)}) copy-start(f32[16,4,24,384]{3,2,1,0:T(8,128)S(1)} %all-to-all-done.part_ref) | copy-start | bytes 7077892

commit v2 on v1

--- a/solution.py
+++ b/solution.py
@@ -1,12 +1,10 @@
-import functools, math
+import functools
 import jax
 import jax.numpy as jnp
 from jax import lax
 from jax.experimental import pallas as pl
 from jax.experimental.pallas import tpu as pltpu
 from jax.sharding import PartitionSpec as P
-
-LOG2E = math.log2(math.e)
 
 
 def look_up(table, index):
@@ -203,6 +201,7 @@
         in_specs=[pl.BlockSpec(memory_space=pltpu.SMEM), pl.BlockSpec(memory_space=pltpu.VMEM)],
         out_specs=pl.BlockSpec(memory_space=pltpu.VMEM),
         out_shape=jax.ShapeDtypeStruct(parts.shape[1:], jnp.float32),
+        compiler_params=pltpu.CompilerParams(vmem_limit_bytes=8 << 20),
         name="x_frame",
     )(order, parts)
 

time: 82.5 us -> 79.9 us (0.968)
  local copies, waits for them, and re-layouts: 2 us -> 0.02 us
  Pallas kernels: 33.5 us -> 32.4 us
    unnamed x4 -> x2, local copies, waits for them, and re-layouts: 1.42 us -> 0.01 us
    pallas_call x1, Pallas kernels: 2.53 us -> 1.4 us  [x_frame(): pl.pallas_call(x_frame_kernel, in_specs=[pl.BlockSpec(memory_space=pltpu....]
  transfers between devices with their start and end apart: 1 -> 1, of which waited for: 1 -> 1; matrix products, arithmetic and copies ran while one was open for 1% -> 0% of each run, Pallas kernels for 26% -> 27%
where the time goes in v2:
time: 79.9 us; the launch traced here: 79.6 us
  Pallas kernels  32.4 us (41%)
  blocking collectives  20.4 us (26%)
  waiting for transfers between devices  15.1 us (19%)
  starting transfers between devices  11 us (14%)
    pallas_call x1, Pallas kernels, yz_views(): pl.pallas_call(functools.partial(yz_kernel, step), grid=(depth, cols // 1...  19.9 us
    all_to_all x1, waiting for transfers between devices, shards(): lax.all_to_all(image_x, 'gx', split_axis=0, concat_axis=0, tiled=True)  15.1 us
    all_gather x1, blocking collectives, shards(): parts_y = lax.all_gather(image_y, 'gy', axis=0)  12.3 us
    all_to_all x1, starting transfers between devices, shards(): lax.all_to_all(image_x, 'gx', split_axis=0, concat_axis=0, tiled=True)  11 us
    pallas_call x1, Pallas kernels, x_view(): pl.pallas_call(functools.partial(x_kernel, step), grid=(pieces // per_ste...  9.42 us
    all_gather x1, blocking collectives, shards(): parts_z = lax.all_gather(image_z, 'gz', axis=0)  8.16 us
    pallas_call x1, Pallas kernels, yz_frames(): pl.pallas_call(yz_frame_kernel, in_specs=[smem, smem, vmem, vmem], out_sp...  1.61 us
  transfers between devices with their start and end apart: 1, of which 1 were waited for; matrix products, arithmetic and copies ran while one was open for 0% of the time, Pallas kernels for 27%

profile of v2, /device:TPU:16, one launch (start us, length us, event | category | flops | bytes accessed | tf_op | source)
XLA Modules:
  0.0 79.6 jit_solution(4863857115000313296)
XLA Ops:
  0.6 0.0 copy-start
  0.6 9.4 %x_view.1 = f32[16,4,24,384]{3,2,1,0:T(8,128)} custom-call(f32[4,384,384]{2,1,0:T(8,128)} %field_ref.3, s32[4,384,384]{2,1,0:T(8,128)} %mark_ref.3, f32[4,128]{1,0:T(4,128)} %transfer_ref.3, f32[4,8]{1,0:T(4,128)} %gain_ref.3), custom_call_target="tpu_custom_call" | custom-call | tf_op jit(solution)/shard_map/x_view/pallas_call | solution.py:71
  10.1 11.0 %all-to-all-start = ((f32[16,4,24,384]{3,2,1,0:T(8,128)}), f32[16,4,24,384]{3,2,1,0:T(8,128)S(1)}, u32[]{:S(2)}, u32[]{:S(2)}) async-start(f32[16,4,24,384]{3,2,1,0:T(8,128)} %x_view.1), calls=%async_computation | async-start | bytes 4718592 | tf_op jit(solution)/shard_map/all_to_all | solution.py:248
  21.1 19.9 %yz_views.1 = (f32[4,4,384]{2,1,0:T(4,128)}, f32[4,4,384]{2,1,0:T(4,128)}) custom-call(f32[4,384,384]{2,1,0:T(8,128)} %field_ref.3, s32[4,384,384]{2,1,0:T(8,128)} %mark_ref.3, f32[4,128]{1,0:T(4,128)} %transfer_ref.3, f32[4,8]{1,0:T(4,128)} %gain_ref.3), custom_call_target="tpu_custom_call" | custom-call | tf_op jit(solution)/shard_map/yz_views/pallas_call | solution.py:159
  41.0 12.3 %all-gather = f32[16,4,384]{2,1,0:T(4,128)} all-gather(f32[4,4,384]{2,1,0:T(4,128)} %get-tuple-element.7), channel_id=2, replica_groups=mesh['gx'=16,'gy'=4,'gz'=4] {'gy'}, dimensions={0}, use_global_device_ids=true | all-gather | bytes 122880 | tf_op jit(solution)/shard_map/all_gather | solution.py:250
  53.3 8.2 %all-gather.1 = f32[16,4,384]{2,1,0:T(4,128)} all-gather(f32[4,4,384]{2,1,0:T(4,128)} %get-tuple-element.8), channel_id=3, replica_groups=mesh['gx'=16,'gy'=4,'gz'=4] {'gz'}, dimensions={0}, use_global_device_ids=true | all-gather | bytes 122880 | tf_op jit(solution)/shard_map/all_gather | solution.py:251
  61.4 1.6 %yz_frames.1 = (f32[4,4,384]{2,1,0:T(4,128)}, f32[4,4,384]{2,1,0:T(4,128)}) custom-call(s32[4]{0:T(128)} %y_order_ref.1, s32[4]{0:T(128)} %z_order_ref.1, f32[4,4,4,384]{3,2,1,0:T(4,128)} %bitcast.7, f32[4,4,4,384]{3,2,1,0:T(4,128)} %bitcast.8), custom_call_target="tpu_custom_call" | custom-call | tf_op jit(solution)/shard_map/yz_frames/pallas_call | solution.py:231
  63.1 0.0 copy-done
  63.1 15.1 %all-to-all-done.part_ref = f32[16,4,24,384]{3,2,1,0:T(8,128)S(1)} async-done(((f32[16,4,24,384]{3,2,1,0:T(8,128)}), f32[16,4,24,384]{3,2,1,0:T(8,128)S(1)}, u32[]{:S(2)}, u32[]{:S(2)}) %all-to-all-start) | async-done | bytes 2359328 | tf_op jit(solution)/shard_map/all_to_all | solution.py:248
  78.2 1.4 %x_frame.1 = f32[4,24,384]{2,1,0:T(8,128)} custom-call(s32[16]{0:T(128)S(1)} %dynamic-slice_bitcast_fusion.order_ref, f32[16,4,24,384]{3,2,1,0:T(8,128)S(1)} %all-to-all-done.part_ref), custom_call_target="tpu_custom_call" | custom-call | tf_op jit(solution)/shard_map/x_frame/pallas_call | solution.py:199
  (1 shorter events, 0.0 us)
Async XLA Ops:
  0.6 62.4 %copy-start = (s32[4,4,16]{2,1,0:T(4,128)S(1)}, s32[4,4,16]{2,1,0:T(4,128)}, u32[]{:S(2)}) copy-start(s32[4,4,16]{2,1,0:T(4,128)} %param.11) | copy-start | bytes 3076
  10.1 68.1 %all-to-all-start = ((f32[16,4,24,384]{3,2,1,0:T(8,128)}), f32[16,4,24,384]{3,2,1,0:T(8,128)S(1)}, u32[]{:S(2)}, u32[]{:S(2)}) async-start(f32[16,4,24,384]{3,2,1,0:T(8,128)} %x_view.1), calls=%async_computation | async-start | bytes 4718592 | tf_op jit(solution)/shard_map/all_to_all | solution.py:248

commit v3 on v2

--- a/solution.py
+++ b/solution.py
@@ -7,6 +7,9 @@
 from jax.sharding import PartitionSpec as P
 
 
+LOG2_E = 1.4426950408889634
+
+
 def look_up(table, index):
     return jnp.take_along_axis(table, index, axis=1, mode="promise_in_bounds")
 
@@ -14,25 +17,38 @@
 def make_tables(transfer_ref, tables_ref):
     bins = transfer_ref.shape[1]
     lane = lax.broadcasted_iota(jnp.int32, (8, 128), 1)
+    values, steps = [], []
     for c in range(4):
         value = jnp.broadcast_to(transfer_ref[pl.ds(c, 1), :], (8, bins))
-        tables_ref[c] = value
-        tables_ref[4 + c] = jnp.where(lane == bins - 1, 0.0, pltpu.roll(value, bins - 1, 1) - value)
-
-
-def classify(cells, marks, tables, gain_ref):
+        step = jnp.where(lane == bins - 1, 0.0, pltpu.roll(value, bins - 1, 1) - value)
+        values.append((value * float(1 << 19) - 0.5).astype(jnp.int32) << 10)
+        steps.append((step * float(1 << 18) + 1048576.0).astype(jnp.int32) - 1048576)
+    for pair in range(2):
+        first, second = 2 * pair, 2 * pair + 1
+        tables_ref[3 * pair] = values[first] | (steps[second] & 1023)
+        tables_ref[3 * pair + 1] = values[second] | 512
+        tables_ref[3 * pair + 2] = (steps[first] << 11) | ((steps[second] >> 10) & 2047)
+
+
+def classify(cells, marks, tables, gain_ref, extinction_scale=1.0):
     scaled = cells * (tables[0].shape[1] - 1.0)
     lower = scaled.astype(jnp.int32)
     fraction = scaled - lower.astype(jnp.float32)
-    values = [look_up(tables[c], lower) for c in range(4)]
-    slopes = [look_up(tables[4 + c], lower) for c in range(4)]
+    words = [look_up(table, lower) for table in tables]
+    samples = []
+    for pair in range(2):
+        first, second, step = words[3 * pair : 3 * pair + 3]
+        samples.append(first.astype(jnp.float32) + fraction * step.astype(jnp.float32))
+        step = (step << 21) | ((first & 1023) << 11)
+        samples.append(second.astype(jnp.float32) + fraction * step.astype(jnp.float32))
     bits = [marks & (1 << k) != 0 for k in range((gain_ref.shape[1] - 1).bit_length())]
     out = []
     for c in range(4):
-        gains = [gain_ref[c, k] for k in range(gain_ref.shape[1])]
+        scale = (extinction_scale if c == 3 else 1.0) / (1 << 29)
+        gains = [gain_ref[c, k] * scale for k in range(gain_ref.shape[1])]
         for bit in bits:
             gains = [jnp.where(bit, high, low) for low, high in zip(gains[0::2], gains[1::2])]
-        out.append((values[c] + fraction * slopes[c]) * gains[0])
+        out.append(samples[c] * gains[0])
     return out
 
 
@@ -41,7 +57,7 @@
     def _():
         make_tables(transfer_ref, tables_ref)
 
-    tables = [tables_ref[k] for k in range(8)]
+    tables = [tables_ref[k] for k in range(6)]
     depth, rows, cols = field_ref.shape
     piece_rows = out_ref.shape[2]
     for piece in range(out_ref.shape[0]):
@@ -50,16 +66,17 @@
                 colour = None
                 for x in range(depth):
                     at = (x, pl.ds(piece * piece_rows + row, 8), pl.ds(col, 128))
-                    red, green, blue, extinction = classify(field_ref[at], mark_ref[at], tables, gain_ref)
-                    passed = jnp.exp(extinction * -step)
-                    opacity = 1.0 - passed
+                    red, green, blue, extinction = classify(field_ref[at], mark_ref[at], tables, gain_ref, -step * LOG2_E)
+                    passed = jnp.exp2(extinction)
                     if colour is None:
-                        colour = [opacity * v for v in (red, green, blue)]
+                        weight = 1.0 - passed
+                        colour = [weight * v for v in (red, green, blue)]
                         through = passed
                     else:
-                        weight = through * opacity
+                        after = through * passed
+                        weight = through - after
                         colour = [a + weight * v for a, v in zip(colour, (red, green, blue))]
-                        through = through * passed
+                        through = after
                 for c, v in enumerate(colour + [through]):
                     out_ref[piece, c, pl.ds(row, 8), pl.ds(col, 128)] = v
 
@@ -79,7 +96,7 @@
         ],
         out_specs=pl.BlockSpec((per_step, 4, piece_rows, cols), lambda i: (i, 0, 0, 0)),
         out_shape=jax.ShapeDtypeStruct((pieces, 4, piece_rows, cols), jnp.float32),
-        scratch_shapes=[pltpu.VMEM((8, 8, 128), jnp.float32)],
+        scratch_shapes=[pltpu.VMEM((6, 8, 128), jnp.int32)],
         name="x_view",
     )(field, marks, transfer_table, material_gain)
 
@@ -116,7 +133,7 @@
     def _():
         make_tables(transfer_ref, tables_ref)
 
-    tables = [tables_ref[k] for k in range(8)]
+    tables = [tables_ref[k] for k in range(6)]
     rows = field_ref.shape[1]
     run = rows // 8
 
@@ -174,7 +191,7 @@
             jax.ShapeDtypeStruct((depth, 4, rows), jnp.float32),
         ],
         scratch_shapes=[
-            pltpu.VMEM((8, 8, 128), jnp.float32),
+            pltpu.VMEM((6, 8, 128), jnp.int32),
             pltpu.VMEM((4, rows, 128), jnp.float32),
             pltpu.VMEM((4, rows // 128, cols, 128), jnp.float32),
         ],

time: 79.9 us -> 79.5 us (level)
  waiting for transfers between devices: 15.1 us -> 17 us
  blocking collectives: 20.4 us -> 19.1 us
  Pallas kernels: 32.4 us -> 31.4 us
    all_to_all x1, waiting for transfers between devices: 15.1 us -> 17 us  [shards(): lax.all_to_all(image_x, 'gx', split_axis=0, concat_axis=0, tiled=True)]
    all_gather x1, blocking collectives: 8.16 us -> 6.8 us  [shards(): parts_z = lax.all_gather(image_z, 'gz', axis=0)]
where the time goes in v3:
time: 79.5 us; the launch traced here: 79.2 us
  Pallas kernels  31.4 us (39%)
  blocking collectives  19.1 us (24%)
  waiting for transfers between devices  17 us (21%)
  starting transfers between devices  11 us (14%)
    pallas_call x1, Pallas kernels, yz_views(): pl.pallas_call(functools.partial(yz_kernel, step), grid=(depth, cols // 1...  19.5 us
    all_to_all x1, waiting for transfers between devices, shards(): lax.all_to_all(image_x, 'gx', split_axis=0, concat_axis=0, tiled=True)  17 us
    all_gather x1, blocking collectives, shards(): parts_y = lax.all_gather(image_y, 'gy', axis=0)  12.3 us
    all_to_all x1, starting transfers between devices, shards(): lax.all_to_all(image_x, 'gx', split_axis=0, concat_axis=0, tiled=True)  11 us
    pallas_call x1, Pallas kernels, x_view(): pl.pallas_call(functools.partial(x_kernel, step), grid=(pieces // per_ste...  8.9 us
    all_gather x1, blocking collectives, shards(): parts_z = lax.all_gather(image_z, 'gz', axis=0)  6.8 us
    pallas_call x1, Pallas kernels, yz_frames(): pl.pallas_call(yz_frame_kernel, in_specs=[smem, smem, vmem, vmem], out_sp...  1.61 us
  transfers between devices with their start and end apart: 1, of which 1 were waited for; matrix products, arithmetic and copies ran while one was open for 0% of the time, Pallas kernels for 27%

profile of v3, /device:TPU:16, one launch (start us, length us, event | category | flops | bytes accessed | tf_op | source)
XLA Modules:
  0.0 79.2 jit_solution(5128041323665027888)
XLA Ops:
  0.6 0.0 copy-start
  0.6 8.9 %x_view.1 = f32[16,4,24,384]{3,2,1,0:T(8,128)} custom-call(f32[4,384,384]{2,1,0:T(8,128)} %field_ref.3, s32[4,384,384]{2,1,0:T(8,128)} %mark_ref.3, f32[4,128]{1,0:T(4,128)} %transfer_ref.3, f32[4,8]{1,0:T(4,128)} %gain_ref.3), custom_call_target="tpu_custom_call" | custom-call | tf_op jit(solution)/shard_map/x_view/pallas_call | solution.py:88
  9.5 11.0 %all-to-all-start = ((f32[16,4,24,384]{3,2,1,0:T(8,128)}), f32[16,4,24,384]{3,2,1,0:T(8,128)S(1)}, u32[]{:S(2)}, u32[]{:S(2)}) async-start(f32[16,4,24,384]{3,2,1,0:T(8,128)} %x_view.1), calls=%async_computation | async-start | bytes 4718592 | tf_op jit(solution)/shard_map/all_to_all | solution.py:265
  20.6 19.5 %yz_views.1 = (f32[4,4,384]{2,1,0:T(4,128)}, f32[4,4,384]{2,1,0:T(4,128)}) custom-call(f32[4,384,384]{2,1,0:T(8,128)} %field_ref.3, s32[4,384,384]{2,1,0:T(8,128)} %mark_ref.3, f32[4,128]{1,0:T(4,128)} %transfer_ref.3, f32[4,8]{1,0:T(4,128)} %gain_ref.3), custom_call_target="tpu_custom_call" | custom-call | tf_op jit(solution)/shard_map/yz_views/pallas_call | solution.py:176
  40.1 12.3 %all-gather = f32[16,4,384]{2,1,0:T(4,128)} all-gather(f32[4,4,384]{2,1,0:T(4,128)} %get-tuple-element.7), channel_id=2, replica_groups=mesh['gx'=16,'gy'=4,'gz'=4] {'gy'}, dimensions={0}, use_global_device_ids=true | all-gather | bytes 122880 | tf_op jit(solution)/shard_map/all_gather | solution.py:267
  52.3 6.8 %all-gather.1 = f32[16,4,384]{2,1,0:T(4,128)} all-gather(f32[4,4,384]{2,1,0:T(4,128)} %get-tuple-element.8), channel_id=3, replica_groups=mesh['gx'=16,'gy'=4,'gz'=4] {'gz'}, dimensions={0}, use_global_device_ids=true | all-gather | bytes 122880 | tf_op jit(solution)/shard_map/all_gather | solution.py:268
  59.1 1.6 %yz_frames.1 = (f32[4,4,384]{2,1,0:T(4,128)}, f32[4,4,384]{2,1,0:T(4,128)}) custom-call(s32[4]{0:T(128)} %y_order_ref.1, s32[4]{0:T(128)} %z_order_ref.1, f32[4,4,4,384]{3,2,1,0:T(4,128)} %bitcast.7, f32[4,4,4,384]{3,2,1,0:T(4,128)} %bitcast.8), custom_call_target="tpu_custom_call" | custom-call | tf_op jit(solution)/shard_map/yz_frames/pallas_call | solution.py:248
  60.8 0.0 copy-done
  60.8 17.0 %all-to-all-done.part_ref = f32[16,4,24,384]{3,2,1,0:T(8,128)S(1)} async-done(((f32[16,4,24,384]{3,2,1,0:T(8,128)}), f32[16,4,24,384]{3,2,1,0:T(8,128)S(1)}, u32[]{:S(2)}, u32[]{:S(2)}) %all-to-all-start) | async-done | bytes 2359328 | tf_op jit(solution)/shard_map/all_to_all | solution.py:265
  77.8 1.4 %x_frame.1 = f32[4,24,384]{2,1,0:T(8,128)} custom-call(s32[16]{0:T(128)S(1)} %dynamic-slice_bitcast_fusion.order_ref, f32[16,4,24,384]{3,2,1,0:T(8,128)S(1)} %all-to-all-done.part_ref), custom_call_target="tpu_custom_call" | custom-call | tf_op jit(solution)/shard_map/x_frame/pallas_call | solution.py:216
  (1 shorter events, 0.0 us)
Async XLA Ops:
  0.6 60.1 %copy-start = (s32[4,4,16]{2,1,0:T(4,128)S(1)}, s32[4,4,16]{2,1,0:T(4,128)}, u32[]{:S(2)}) copy-start(s32[4,4,16]{2,1,0:T(4,128)} %param.11) | copy-start | bytes 3076
  9.5 68.2 %all-to-all-start = ((f32[16,4,24,384]{3,2,1,0:T(8,128)}), f32[16,4,24,384]{3,2,1,0:T(8,128)S(1)}, u32[]{:S(2)}, u32[]{:S(2)}) async-start(f32[16,4,24,384]{3,2,1,0:T(8,128)} %x_view.1), calls=%async_computation | async-start | bytes 4718592 | tf_op jit(solution)/shard_map/all_to_all | solution.py:265

commit v4 on v3

--- a/solution.py
+++ b/solution.py
@@ -23,7 +23,10 @@
         step = jnp.where(lane == bins - 1, 0.0, pltpu.roll(value, bins - 1, 1) - value)
         values.append((value * float(1 << 19) - 0.5).astype(jnp.int32) << 10)
         steps.append((step * float(1 << 18) + 1048576.0).astype(jnp.int32) - 1048576)
-    for pair in range(2):
+    for c in (2, 3):
+        tables_ref[c + 1] = values[c]
+        tables_ref[c + 3] = steps[c] << 11
+    for pair in range(1):
         first, second = 2 * pair, 2 * pair + 1
         tables_ref[3 * pair] = values[first] | (steps[second] & 1023)
         tables_ref[3 * pair + 1] = values[second] | 512
@@ -36,11 +39,13 @@
     fraction = scaled - lower.astype(jnp.float32)
     words = [look_up(table, lower) for table in tables]
     samples = []
-    for pair in range(2):
+    for pair in range(1):
         first, second, step = words[3 * pair : 3 * pair + 3]
         samples.append(first.astype(jnp.float32) + fraction * step.astype(jnp.float32))
         step = (step << 21) | ((first & 1023) << 11)
         samples.append(second.astype(jnp.float32) + fraction * step.astype(jnp.float32))
+    for value, step in zip(words[3:5], words[5:7]):
+        samples.append(value.astype(jnp.float32) + fraction * step.astype(jnp.float32))
     bits = [marks & (1 << k) != 0 for k in range((gain_ref.shape[1] - 1).bit_length())]
     out = []
     for c in range(4):
@@ -57,7 +62,7 @@
     def _():
         make_tables(transfer_ref, tables_ref)
 
-    tables = [tables_ref[k] for k in range(6)]
+    tables = [tables_ref[k] for k in range(7)]
     depth, rows, cols = field_ref.shape
     piece_rows = out_ref.shape[2]
     for piece in range(out_ref.shape[0]):
@@ -96,7 +101,7 @@
         ],
         out_specs=pl.BlockSpec((per_step, 4, piece_rows, cols), lambda i: (i, 0, 0, 0)),
         out_shape=jax.ShapeDtypeStruct((pieces, 4, piece_rows, cols), jnp.float32),
-        scratch_shapes=[pltpu.VMEM((6, 8, 128), jnp.int32)],
+        scratch_shapes=[pltpu.VMEM((7, 8, 128), jnp.int32)],
         name="x_view",
     )(field, marks, transfer_table, material_gain)
 
@@ -133,7 +138,7 @@
     def _():
         make_tables(transfer_ref, tables_ref)
 
-    tables = [tables_ref[k] for k in range(6)]
+    tables = [tables_ref[k] for k in range(7)]
     rows = field_ref.shape[1]
     run = rows // 8
 
@@ -191,7 +196,7 @@
             jax.ShapeDtypeStruct((depth, 4, rows), jnp.float32),
         ],
         scratch_shapes=[
-            pltpu.VMEM((6, 8, 128), jnp.int32),
+            pltpu.VMEM((7, 8, 128), jnp.int32),
             pltpu.VMEM((4, rows, 128), jnp.float32),
             pltpu.VMEM((4, rows // 128, cols, 128), jnp.float32),
         ],

time: 79.5 us -> 79.4 us (level)
  waiting for transfers between devices: 17 us -> 14.5 us
  Pallas kernels: 31.4 us -> 32.7 us
  blocking collectives: 19.1 us -> 20.2 us
    all_to_all x1, waiting for transfers between devices: 17 us -> 14.5 us  [shards(): lax.all_to_all(image_x, 'gx', split_axis=0, concat_axis=0, tiled=True)]
    pallas_call x1, Pallas kernels: 19.5 us -> 20.8 us  [yz_views(): pl.pallas_call(functools.partial(yz_kernel, step), grid=(depth, cols // 1...]
    all_gather x1, blocking collectives: 6.8 us -> 7.9 us  [shards(): parts_z = lax.all_gather(image_z, 'gz', axis=0)]
  transfers between devices with their start and end apart: 1 -> 1, of which waited for: 1 -> 1; matrix products, arithmetic and copies ran while one was open for 0% -> 0% of each run, Pallas kernels for 27% -> 28%
where the time goes in v4:
time: 79.4 us; the launch traced here: 79.1 us
  Pallas kernels  32.7 us (41%)
  blocking collectives  20.2 us (25%)
  waiting for transfers between devices  14.5 us (18%)
  starting transfers between devices  11 us (14%)
    pallas_call x1, Pallas kernels, yz_views(): pl.pallas_call(functools.partial(yz_kernel, step), grid=(depth, cols // 1...  20.8 us
    all_to_all x1, waiting for transfers between devices, shards(): lax.all_to_all(image_x, 'gx', split_axis=0, concat_axis=0, tiled=True)  14.5 us
    all_gather x1, blocking collectives, shards(): parts_y = lax.all_gather(image_y, 'gy', axis=0)  12.3 us
    all_to_all x1, starting transfers between devices, shards(): lax.all_to_all(image_x, 'gx', split_axis=0, concat_axis=0, tiled=True)  11 us
    pallas_call x1, Pallas kernels, x_view(): pl.pallas_call(functools.partial(x_kernel, step), grid=(pieces // per_ste...  8.92 us
    all_gather x1, blocking collectives, shards(): parts_z = lax.all_gather(image_z, 'gz', axis=0)  7.9 us
    pallas_call x1, Pallas kernels, yz_frames(): pl.pallas_call(yz_frame_kernel, in_specs=[smem, smem, vmem, vmem], out_sp...  1.61 us
  transfers between devices with their start and end apart: 1, of which 1 were waited for; matrix products, arithmetic and copies ran while one was open for 0% of the time, Pallas kernels for 28%

profile of v4, /device:TPU:16, one launch (start us, length us, event | category | flops | bytes accessed | tf_op | source)
XLA Modules:
  0.0 79.1 jit_solution(5123676083176522233)
XLA Ops:
  0.6 0.0 copy-start
  0.6 8.9 %x_view.1 = f32[16,4,24,384]{3,2,1,0:T(8,128)} custom-call(f32[4,384,384]{2,1,0:T(8,128)} %field_ref.3, s32[4,384,384]{2,1,0:T(8,128)} %mark_ref.3, f32[4,128]{1,0:T(4,128)} %transfer_ref.3, f32[4,8]{1,0:T(4,128)} %gain_ref.3), custom_call_target="tpu_custom_call" | custom-call | tf_op jit(solution)/shard_map/x_view/pallas_call | solution.py:93
  9.6 11.0 %all-to-all-start = ((f32[16,4,24,384]{3,2,1,0:T(8,128)}), f32[16,4,24,384]{3,2,1,0:T(8,128)S(1)}, u32[]{:S(2)}, u32[]{:S(2)}) async-start(f32[16,4,24,384]{3,2,1,0:T(8,128)} %x_view.1), calls=%async_computation | async-start | bytes 4718592 | tf_op jit(solution)/shard_map/all_to_all | solution.py:270
  20.6 20.8 %yz_views.1 = (f32[4,4,384]{2,1,0:T(4,128)}, f32[4,4,384]{2,1,0:T(4,128)}) custom-call(f32[4,384,384]{2,1,0:T(8,128)} %field_ref.3, s32[4,384,384]{2,1,0:T(8,128)} %mark_ref.3, f32[4,128]{1,0:T(4,128)} %transfer_ref.3, f32[4,8]{1,0:T(4,128)} %gain_ref.3), custom_call_target="tpu_custom_call" | custom-call | tf_op jit(solution)/shard_map/yz_views/pallas_call | solution.py:181
  41.4 12.3 %all-gather = f32[16,4,384]{2,1,0:T(4,128)} all-gather(f32[4,4,384]{2,1,0:T(4,128)} %get-tuple-element.7), channel_id=2, replica_groups=mesh['gx'=16,'gy'=4,'gz'=4] {'gy'}, dimensions={0}, use_global_device_ids=true | all-gather | bytes 122880 | tf_op jit(solution)/shard_map/all_gather | solution.py:272
  53.6 7.9 %all-gather.1 = f32[16,4,384]{2,1,0:T(4,128)} all-gather(f32[4,4,384]{2,1,0:T(4,128)} %get-tuple-element.8), channel_id=3, replica_groups=mesh['gx'=16,'gy'=4,'gz'=4] {'gz'}, dimensions={0}, use_global_device_ids=true | all-gather | bytes 122880 | tf_op jit(solution)/shard_map/all_gather | solution.py:273
  61.5 1.6 %yz_frames.1 = (f32[4,4,384]{2,1,0:T(4,128)}, f32[4,4,384]{2,1,0:T(4,128)}) custom-call(s32[4]{0:T(128)} %y_order_ref.1, s32[4]{0:T(128)} %z_order_ref.1, f32[4,4,4,384]{3,2,1,0:T(4,128)} %bitcast.7, f32[4,4,4,384]{3,2,1,0:T(4,128)} %bitcast.8), custom_call_target="tpu_custom_call" | custom-call | tf_op jit(solution)/shard_map/yz_frames/pallas_call | solution.py:253
  63.2 0.0 copy-done
  63.2 14.5 %all-to-all-done.part_ref = f32[16,4,24,384]{3,2,1,0:T(8,128)S(1)} async-done(((f32[16,4,24,384]{3,2,1,0:T(8,128)}), f32[16,4,24,384]{3,2,1,0:T(8,128)S(1)}, u32[]{:S(2)}, u32[]{:S(2)}) %all-to-all-start) | async-done | bytes 2359328 | tf_op jit(solution)/shard_map/all_to_all | solution.py:270
  77.6 1.4 %x_frame.1 = f32[4,24,384]{2,1,0:T(8,128)} custom-call(s32[16]{0:T(128)S(1)} %dynamic-slice_bitcast_fusion.order_ref, f32[16,4,24,384]{3,2,1,0:T(8,128)S(1)} %all-to-all-done.part_ref), custom_call_target="tpu_custom_call" | custom-call | tf_op jit(solution)/shard_map/x_frame/pallas_call | solution.py:221
  (1 shorter events, 0.0 us)
Async XLA Ops:
  0.6 62.5 %copy-start = (s32[4,4,16]{2,1,0:T(4,128)S(1)}, s32[4,4,16]{2,1,0:T(4,128)}, u32[]{:S(2)}) copy-start(s32[4,4,16]{2,1,0:T(4,128)} %param.11) | copy-start | bytes 3076
  9.6 68.1 %all-to-all-start = ((f32[16,4,24,384]{3,2,1,0:T(8,128)}), f32[16,4,24,384]{3,2,1,0:T(8,128)S(1)}, u32[]{:S(2)}, u32[]{:S(2)}) async-start(f32[16,4,24,384]{3,2,1,0:T(8,128)} %x_view.1), calls=%async_computation | async-start | bytes 4718592 | tf_op jit(solution)/shard_map/all_to_all | solution.py:270
